TPU v7x, 128 devices: a whole 4x4x4 slice. The times are simulated.
128 devices in a mesh: rep: 8 (over y, z_lo), tp: 16 (over x, z_hi, core).
Axes of the slice: x: 4, y: 4, z: 4 (z_hi: 2, z_lo: 2; z = z_hi * 2 + z_lo), core: 2. Of those that a mesh axis runs over, the one named last changes fastest.
Arguments:
- embeds: bfloat16 [6272, 5120], P('rep', 'tp'), parts along dimension 0, may hold values from -6 to 6
- remask: int32 [6272], P('rep'), parts along dimension 0, may hold values 0 or 1
- lengths: int32 [32], P('rep'), parts along dimension 0, may hold values from 49 to 196, as said below
- mask_vec: bfloat16 [5120], P('tp'), may hold values from -6 to 6
- attn_gain: bfloat16 [5120], replicated, may hold values from 0.25 to 1.75
- w_query: bfloat16 [5120, 4096], P(None, 'tp'), may hold values from -0.078125 to 0.078125
- q_bias: bfloat16 [4096], P('tp'), may hold values from -200 to 200
- w_key: bfloat16 [5120, 1024], P(None, 'tp'), may hold values from -0.078125 to 0.078125
- w_value: bfloat16 [5120, 1024], P(None, 'tp'), may hold values from -0.078125 to 0.078125
- v_bias: bfloat16 [1024], P('tp'), may hold values from -3 to 3
- w_out: bfloat16 [4096, 5120], P('tp'), may hold values from -0.125 to 0.125
- head_gain: bfloat16 [5120], replicated, may hold values from 0.25 to 1.75
- w_head: bfloat16 [5120, 512], P(None, 'tp'), may hold values from -20 to 20
Outputs:
- hidden: bfloat16 [6272, 5120], P('rep', 'tp'), parts along dimension 0
- logprob: float32 [6272, 512], P('rep', 'tp'), parts along dimension 0
There are 8 independent parts, one for each index of `rep`. A program takes and returns all parts, laid end to end along the dimension named above; an argument that names none is the same for every part. Nothing has to cross between parts.
Inputs may be any that keep to these rules, and one draw needn't show every extreme that they name: `lengths`: every request has at least 49 tokens, and one request of each part has exactly 196.
All inputs are finite; a program needn't handle non-finite values.
Results may differ from a plain program's by a relative error of at most 0.018.
The roundings to bfloat16 on the way count: a program that leaves them out, or rounds other values in their place, can miss the bound.
Values may be sent and summed in bfloat16 or wider, within the bound.
A program may use at most 128 MiB of HBM per device.

v0:
```python
import jax
import jax.numpy as jnp
from jax import lax
from jax.sharding import PartitionSpec as P

HS = 128
L = 196


EPS = 1e-06


def swapped(value, axis, apart):
    mask = 2**apart
    pairs = [(source, source ^ mask) for source in range(lax.axis_size(axis))]
    return lax.ppermute(value, axis, pairs)


def combined_all(x, axis, combine):
    everything = jax.tree.map(lambda part: lax.all_gather(part, axis), x)
    initial = jax.tree.map(lambda part: part[0], everything)

    def lap(k, so_far):
        return combine(so_far, jax.tree.map(lambda part: part[k], everything))

    return lax.fori_loop(1, lax.axis_size(axis), lap, initial)


def rms_norm(matrix, gain):
    wide = matrix.astype(jnp.float32)
    inverse = lax.rsqrt(jnp.mean(wide * wide, axis=-1, keepdims=True) + EPS)
    return (wide * inverse * gain.astype(jnp.float32)).astype(jnp.bfloat16)


def combine_pair(first_pair, second_pair):
    top = jnp.maximum(first_pair[0], second_pair[0])
    total = first_pair[1] * jnp.exp(first_pair[0] - top) + second_pair[1] * jnp.exp(
        second_pair[0] - top
    )
    return (top, total)


def on_device(
    embeds,
    remask,
    lengths,
    mask_vec,
    attn_gain,
    w_query,
    q_bias,
    w_key,
    w_value,
    v_bias,
    w_out,
    head_gain,
    w_head,
):
    requests = lengths.shape[0]
    tokens_all = embeds.shape[0]
    masked_local = jnp.where(remask[:, None] == 1, mask_vec[None, :], embeds)
    gathered = lax.all_gather(masked_local, "tp", axis=1, tiled=True)
    normed = rms_norm(gathered, attn_gain)
    queries = (
        jnp.dot(normed, w_query, preferred_element_type=jnp.float32) + q_bias.astype(jnp.float32)
    ).astype(jnp.bfloat16)
    key_rows = jnp.dot(normed, w_key, preferred_element_type=jnp.float32).astype(jnp.bfloat16)
    value_rows = (
        jnp.dot(normed, w_value, preferred_element_type=jnp.float32) + v_bias.astype(jnp.float32)
    ).astype(jnp.bfloat16)
    my_index = lax.axis_index("tp")
    other_key, other_value = swapped((key_rows, value_rows), "tp", 0)
    lower = jnp.bitwise_and(jnp.right_shift(my_index, 0), 1) == 0
    key_rows = jnp.where(
        lower,
        jnp.concatenate([key_rows, other_key], axis=1),
        jnp.concatenate([other_key, key_rows], axis=1),
    )
    value_rows = jnp.where(
        lower,
        jnp.concatenate([value_rows, other_value], axis=1),
        jnp.concatenate([other_value, value_rows], axis=1),
    )
    heads_dev = queries.shape[1] // HS
    kv_count = key_rows.shape[1] // HS
    repeats = heads_dev // kv_count
    k_four = jnp.repeat(key_rows.reshape(requests, L, kv_count, HS), repeats, axis=2)
    v_four = jnp.repeat(value_rows.reshape(requests, L, kv_count, HS), repeats, axis=2)
    q_four = queries.reshape(requests, L, heads_dev, HS)
    scores = jnp.einsum(
        "rqhd,rkhd->rhqk", q_four, k_four, preferred_element_type=jnp.float32
    ) * HS ** (-0.5)
    valid = jnp.arange(L, dtype=jnp.int32)[None, :] < lengths[:, None]
    scores = jnp.where(valid[:, None, None, :], scores, jnp.float32(-1e30))
    peak = jnp.max(scores, axis=-1, keepdims=True)
    expo = jnp.exp(scores - peak)
    attn_prob = (expo / jnp.sum(expo, axis=-1, keepdims=True)).astype(jnp.bfloat16)
    context = jnp.einsum(
        "rhqk,rkhd->rqhd", attn_prob, v_four, preferred_element_type=jnp.float32
    ).astype(jnp.bfloat16)
    context = context.reshape(tokens_all, heads_dev * HS)
    portion = lax.psum_scatter(
        lax.dot_general(
            w_out, context, (((0,), (1,)), ((), ())), preferred_element_type=jnp.float32
        ).astype(jnp.bfloat16),
        "tp",
        scatter_dimension=0,
        tiled=True,
    ).astype(jnp.float32)
    hidden_local = (masked_local.astype(jnp.float32) + portion.T).astype(jnp.bfloat16)
    hidden_full = lax.all_gather(hidden_local, "tp", axis=1, tiled=True)
    normed_head = rms_norm(hidden_full, head_gain)
    logits = jnp.dot(normed_head, w_head, preferred_element_type=jnp.float32)
    local_top = jnp.max(logits, axis=-1)
    local_total = jnp.sum(jnp.exp(logits - local_top[:, None]), axis=-1)
    row_top, row_total = combined_all((local_top, local_total), "tp", combine_pair)
    log_total = row_top + jnp.log(row_total)
    return (hidden_local, logits - log_total[:, None])


def solution(mesh):
    placed = (
        P("rep", "tp"),
        P("rep"),
        P("rep"),
        P("tp"),
        P(),
        P(None, "tp"),
        P("tp"),
        P(None, "tp"),
        P(None, "tp"),
        P("tp"),
        P("tp", None),
        P(),
        P(None, "tp"),
    )
    return jax.shard_map(
        on_device,
        mesh=mesh,
        in_specs=placed,
        out_specs=(P("rep", "tp"), P("rep", "tp")),
        check_vma=False,
    )
```

profile of v0, /device:TPU:1, one launch (start us, length us, event | category | flops | bytes accessed | tf_op | source)
XLA Modules:
  0.0 478.1 jit_solution(16068774313407309099)
XLA Ops:
  7.2 0.0 copy-start
  7.2 0.0 all-gather.5.cloned.1.call-start
  7.2 0.8 broadcast_compare_fusion
  8.1 2.0 broadcast_select_fusion
  10.1 0.0 all-gather.5.cloned.1.call-update
  10.1 0.0 reduce-scatter.4.cloned.1.call-start
  10.1 0.7 convert_element_type.57
  10.9 0.7 convert_element_type.59
  11.5 0.7 convert_element_type.61
  12.2 0.7 iota_compare_fusion
  12.9 77.8 %all-gather.5.cloned.1.call-done = bf16[784,5120]{0,1:T(8,128)(2,1)} async-done(((bf16[784,320]{0,1:T(8,128)(2,1)}), bf16[784,5120]{0,1:T(8,128)(2,1)}) %all-gather.5.cloned.1.call-update) | async-done | bytes 8028176 | tf_op jit(solution)/shard_map/all_gather | solution.py:61
  90.7 5.5 %fusion.1 = f32[784]{0:T(1024)S(1)} fusion(bf16[784,5120]{0,1:T(8,128)(2,1)} %all-gather.5.cloned.1.call-done), kind=kLoop, calls=%fused_computation.8 | loop fusion | flops 12041456 | bytes 8031296 | tf_op jit(solution)/shard_map/reduce_sum | solution.py:31
  96.2 0.0 copy-start.5
  96.2 9.4 %fusion.3 = bf16[784,5120]{0,1:T(8,128)(2,1)} fusion(bf16[784,5120]{0,1:T(8,128)(2,1)} %all-gather.5.cloned.1.call-done, f32[5120]{0:T(1024)S(1)} %convert_element_type.57, f32[784]{0:T(1024)S(1)} %add_rsqrt_fusion.1), kind=kLoop, calls=%fused_computation.10 | loop fusion | flops 16056320 | bytes 16079936 | tf_op jit(solution)/shard_map/convert_element_type | solution.py:32
  105.6 0.0 copy-done.5
  105.6 5.3 %fusion.15 = bf16[784,64]{0,1:T(8,128)(2,1)S(1)} fusion(bf16[5120,64]{0,1:T(8,128)(2,1)S(1)} %copy-done.5, bf16[784,5120]{0,1:T(8,128)(2,1)} %fusion.3, f32[64]{0:T(128)S(1)} %convert_element_type.59), kind=kOutput, calls=%fused_computation.28 | convolution fusion | flops 513902592 | bytes 8784128 | tf_op jit(solution)/shard_map/dot_general | solution.py:68
  110.9 0.0 copy-start.3
  110.9 0.3 collective-permute-start
  111.2 0.6 copy-done.1
  111.8 0.1 copy-done.6
  111.9 1.5 convolution_convert_fusion.2
  113.5 0.5 collective-permute-start.1
  114.0 0.0 copy-done.3
  114.0 2.6 fusion.13
  116.6 0.1 concatenate.28
  116.8 0.1 concatenate.32
  116.9 0.8 reshape.89
  117.8 0.0 collective-permute-done
  117.8 1.0 concatenate.29
  118.8 0.0 collective-permute-done.1
  118.8 1.7 concatenate.33
  120.5 1.6 maximum_select_fusion
  122.1 0.2 copy.29
  122.4 0.2 copy.28
  122.6 2.9 exponential_reduce_fusion
  125.5 1.9 fusion.14
  127.4 0.3 copy.32
  127.7 0.0 copy-done
  127.7 5.4 %fusion.11 = bf16[5120,784]{0,1:T(8,128)(2,1)} fusion(bf16[256,5120]{1,0:T(8,128)(2,1)S(1)} %copy-done, bf16[98,8,2,128]{3,2,1,0:T(2,128)(2,1)S(1)} %bitcast.31), kind=kOutput, calls=%fused_computation.18 | convolution fusion | flops 2059223040 | bytes 11051008 | tf_op jit(solution)/shard_map/dot_general | solution.py:102
  133.1 12.6 %copy.35 = bf16[5120,784]{1,0:T(8,128)(2,1)} copy(bf16[5120,784]{0,1:T(8,128)(2,1)} %fusion.11) | data formatting | bytes 16056320
  145.7 0.0 reduce-scatter.4.cloned.1.call-update
  145.7 0.0 all-gather.7.cloned.1.call-start
  145.8 102.2 %reduce-scatter.4.cloned.1.call-done = bf16[320,784]{1,0:T(8,128)(2,1)} async-done(((bf16[5120,784]{1,0:T(8,128)(2,1)}), bf16[320,784]{1,0:T(8,128)(2,1)}) %reduce-scatter.4.cloned.1.call-update) | async-done | bytes 501776 | tf_op jit(solution)/shard_map/reduce_scatter | solution.py:101
  248.0 0.0 copy-done.10
  248.0 2.1 fusion.16
  250.1 0.0 all-gather.7.cloned.1.call-update
  250.1 0.3 all-reduce.5.cloned.1.call-start
  250.4 0.6 dynamic-slice
  251.7 75.6 %all-gather.7.cloned.1.call-done = bf16[784,5120]{0,1:T(8,128)(2,1)} async-done(((bf16[784,320]{0,1:T(8,128)(2,1)}), bf16[784,5120]{0,1:T(8,128)(2,1)}) %all-gather.7.cloned.1.call-update) | async-done | bytes 8028176 | tf_op jit(solution)/shard_map/all_gather | solution.py:110
  327.3 5.7 %fusion.4 = f32[784]{0:T(1024)S(1)} fusion(bf16[784,5120]{0,1:T(8,128)(2,1)} %all-gather.7.cloned.1.call-done), kind=kLoop, calls=%fused_computation.11 | loop fusion | flops 12041456 | bytes 8031296 | tf_op jit(solution)/shard_map/reduce_sum | solution.py:31
  333.0 0.5 copy-done.2
  333.5 2.7 fusion.37
  336.3 0.3 dynamic-update-slice
  336.6 0.3 dynamic-update-slice.1
  336.9 0.3 copy-done.8
  337.2 0.3 copy-done.7
  337.5 0.0 all-reduce.5.cloned.1.call-update
  337.5 129.1 %all-reduce.5.cloned.1.call-done = (f32[12544]{0:T(1024)}, f32[12544]{0:T(1024)}) async-done(((f32[12544]{0:T(1024)}, f32[12544]{0:T(1024)}), (f32[12544]{0:T(1024)}, f32[12544]{0:T(1024)})) %all-reduce.5.cloned.1.call-update) | async-done | bytes 100368
  466.6 0.9 reshape.92
  467.5 0.7 slice.10
  468.2 0.9 reshape.93
  469.1 0.7 slice.11
  469.8 1.1 while.17
  470.9 0.7 broadcast_subtract_fusion
  (51 shorter events, 0.7 us)
Async XLA Ops:
  7.2 120.6 %copy-start = (bf16[256,5120]{1,0:T(8,128)(2,1)S(1)}, bf16[256,5120]{1,0:T(8,128)(2,1)}, u32[]{:S(2)}) copy-start(bf16[256,5120]{1,0:T(8,128)(2,1)} %param.25) | copy-start | bytes 7864324
  7.2 83.5 %all-gather.5.cloned.1.call-start = ((), (), s32[]{:S(2)}) async-start(), calls=%async_computation.1 | async-start | bytes 9748480 | tf_op jit(solution)/shard_map/all_gather | solution.py:61
  10.1 237.9 %reduce-scatter.4.cloned.1.call-start = ((), (), s32[]{:S(2)}) async-start(), calls=%async_computation.3 | async-start | bytes 9748480 | tf_op jit(solution)/shard_map/reduce_scatter | solution.py:101
  96.2 9.4 %copy-start.5 = (bf16[5120,64]{0,1:T(8,128)(2,1)S(1)}, bf16[5120,64]{0,1:T(8,128)(2,1)}, u32[]{:S(2)}) copy-start(bf16[5120,64]{0,1:T(8,128)(2,1)} %param.23) | copy-start | bytes 1966084
  105.6 6.2 %copy-start.1 = (bf16[784,5120]{0,1:T(8,128)(2,1)S(1)}, bf16[784,5120]{0,1:T(8,128)(2,1)}, u32[]{:S(2)}) copy-start(bf16[784,5120]{0,1:T(8,128)(2,1)} %fusion.3) | copy-start | bytes 24084484
  105.6 6.3 %copy-start.6 = (bf16[5120,64]{0,1:T(8,128)(2,1)S(1)}, bf16[5120,64]{0,1:T(8,128)(2,1)}, u32[]{:S(2)}) copy-start(bf16[5120,64]{0,1:T(8,128)(2,1)} %param.22) | copy-start | bytes 1966084
  110.9 3.1 copy-start.3
  110.9 6.8 %collective-permute-start = (bf16[784,64]{0,1:T(8,128)(2,1)S(1)}, bf16[784,64]{0,1:T(8,128)(2,1)}, u32[]{:S(2)}, u32[]{:S(2)}) collective-permute-start(bf16[784,64]{0,1:T(8,128)(2,1)S(1)} %fusion.15), channel_id=1, source_target_pairs={{0,1},{1,0},{2,3},{3,2},{4,5},{5,4},{6,7},{7,6},{8,9},{9,8},{10,11... | collective-permute-start | bytes 301064 | tf_op jit(solution)/shard_map/ppermute | solution.py:16
  113.5 5.4 %collective-permute-start.1 = (bf16[784,64]{0,1:T(8,128)(2,1)S(1)}, bf16[784,64]{0,1:T(8,128)(2,1)}, u32[]{:S(2)}, u32[]{:S(2)}) collective-permute-start(bf16[784,64]{0,1:T(8,128)(2,1)S(1)} %convolution_convert_fusion.2), channel_id=1, source_target_pairs={{0,1},{1,0},{2,3},{3,2},{4,5},{5,4},{6,7},{7,6},{8,9},{9,8},{10,11... | collective-permute-start | bytes 301064 | tf_op jit(solution)/shard_map/ppermute | solution.py:16
  133.1 114.9 %copy-start.4 = (bf16[784,320]{0,1:T(8,128)(2,1)S(1)}, bf16[784,320]{0,1:T(8,128)(2,1)}, u32[]{:S(2)}) copy-start(bf16[784,320]{0,1:T(8,128)(2,1)} %param.15) | copy-start | bytes 1505284
  133.1 114.9 %copy-start.10 = (bf16[320]{0:T(512)(128)(2,1)S(1)}, bf16[320]{0:T(512)(128)(2,1)}, u32[]{:S(2)}) copy-start(bf16[320]{0:T(512)(128)(2,1)} %param.18) | copy-start | bytes 1924
  145.7 104.7 %copy-start.9 = (bf16[5120]{0:T(1024)(128)(2,1)S(1)}, bf16[5120]{0:T(1024)(128)(2,1)}, u32[]{:S(2)}) copy-start(bf16[5120]{0:T(1024)(128)(2,1)} %param.26) | copy-start | bytes 30724
  145.7 104.7 %copy-start.12 = (u32[128]{0:T(128)S(1)}, u32[128]{0:T(128)}, u32[]{:S(2)}) copy-start(u32[128]{0:T(128)} %constant.61) | copy-start | bytes 1540
  145.7 187.3 %copy-start.11 = (bf16[5120,32]{0,1:T(8,128)(2,1)S(1)}, bf16[5120,32]{0,1:T(8,128)(2,1)}, u32[]{:S(2)}) copy-start(bf16[5120,32]{0,1:T(8,128)(2,1)} %param.27) | copy-start | bytes 983044
  145.7 181.5 %all-gather.7.cloned.1.call-start = ((), (), s32[]{:S(2)}) async-start(), calls=%async_computation.2 | async-start | bytes 9748480 | tf_op jit(solution)/shard_map/all_gather | solution.py:110
  250.1 216.5 %all-reduce.5.cloned.1.call-start = ((), (), s32[]{:S(2)}) async-start(), calls=%async_computation.4 | async-start | bytes 212992
  327.3 6.2 %copy-start.2 = (bf16[784,5120]{0,1:T(8,128)(2,1)S(1)}, bf16[784,5120]{0,1:T(8,128)(2,1)}, u32[]{:S(2)}) copy-start(bf16[784,5120]{0,1:T(8,128)(2,1)} %all-gather.7.cloned.1.call-done) | copy-start | bytes 24084484
  336.6 0.6 copy-start.8
  336.9 0.6 copy-start.7
Sparse Core Ops, SparseCore 0:
  11.0 79.6 all-gather.4
  145.9 102.0 reduce-scatter.3
  251.0 76.2 all-gather.6
  337.6 128.9 all-reduce.4
where the time goes:
time: 479 us; the launch traced here: 478 us
  waiting for transfers between devices  385 us (80%)
  other arithmetic  30.8 us (6%)
  local copies, waits for them, and re-layouts  23.9 us (5%)
  matrix products  22.3 us (5%)
  between operations  14.6 us (3%)
    unnamed x5, waiting for transfers between devices  129 us
    reduce_scatter x1, waiting for transfers between devices, on_device(): lax.psum_scatter(lax.dot_general(w_out, context, (((0,), (1,)), ((), ()))...  102 us
    all_gather x1, waiting for transfers between devices, on_device(): gathered = lax.all_gather(masked_local, 'tp', axis=1, tiled=True)  77.8 us
    all_gather x1, waiting for transfers between devices, on_device(): hidden_full = lax.all_gather(hidden_local, 'tp', axis=1, tiled=True)  75.6 us
    unnamed x32, local copies, waits for them, and re-layouts  15.6 us
    reduce_sum x2, other arithmetic, rms_norm(): inverse = lax.rsqrt(jnp.mean(wide * wide, axis=-1, keepdims=True) + EPS)  11.2 us
    convert_element_type x3, other arithmetic, rms_norm(): return (wide * inverse * gain.astype(jnp.float32)).astype(jnp.bfloat16)  10.1 us
  transfers between devices with their start and end apart: 6, of which 4 were waited for; matrix products, arithmetic and copies ran while one was open for 2% of the time, Pallas kernels for 0%

commit v1 on v0

v1 whole, which is shorter than its diff:
```python
import jax
import jax.numpy as jnp
from jax import lax
from jax.experimental import pallas as pl
from jax.experimental.pallas import tpu as pltpu
from jax.sharding import PartitionSpec as P

HS = 128
L = 196
ROWS = 200
LANES = 256
CHIPS = 8
WIDE = 640
D = 5120
HALF = 320
EPS = 1e-06
MESH = pl.DeviceIdType.MESH
F32 = jnp.float32
BF16 = jnp.bfloat16

SIB_X, SIB_WQ, SIB_WK, SIB_WV, SIB_WO, SIB_SMALL, SIB_HEAD = 0, 2, 3, 4, 5, 6, 7
AG = 8
RS = AG + 14
HEAD = RS + 14
LOGIT = HEAD + 7
STAT = LOGIT + 14
SIB_HID = STAT + 14
SIB_LP = SIB_HID + 2
COPIES = SIB_LP + 2


def dot_nt(a, b):
    return lax.dot_general(a, b, (((1,), (1,)), ((), ())), preferred_element_type=F32)


def kernel(
    lengths,
    x4,
    small,
    gains,
    wq_in,
    wk_in,
    wv_in,
    wo_in,
    wh_in,
    hid_out,
    lp_out,
    sib_x,
    xg,
    wq,
    wkv,
    wo,
    whp,
    whg,
    sm,
    acc_q,
    acc_kv,
    q_ref,
    k_ref,
    v_ref,
    ctx,
    stage,
    got,
    hid,
    hid_send,
    lmsg,
    lgot,
    smsg,
    sgot,
    lp_send,
    ssem,
    rsem,
    lsem,
):
    me = lax.axis_index("tp")
    x = me // 4
    zh = lax.rem(me // 2, 2)
    c = lax.rem(me, 2)
    chip = me // 2
    zo = 1 - zh
    xp, xm, xx = lax.rem(x + 1, 4), lax.rem(x + 3, 4), lax.rem(x + 2, 4)

    def core(xs, zs):
        return {"tp": xs * 4 + zs * 2 + c}

    def block(xs, zs):
        return xs * 2 + zs

    sibling = {"tp": me + 1 - 2 * c}
    others = [lax.rem(chip + d, CHIPS) for d in range(1, CHIPS)]
    started = []

    def send(number, src, dst, target):
        copy = pltpu.make_async_remote_copy(
            src_ref=src,
            dst_ref=dst,
            send_sem=ssem.at[number],
            recv_sem=rsem.at[number],
            device_id=target,
            device_id_type=MESH,
        )
        copy.start()
        started.append(copy)
        return copy

    barrier = pltpu.get_barrier_semaphore()
    pl.semaphore_signal(barrier, inc=1, device_id=sibling, device_id_type=MESH)
    for other in others:
        pl.semaphore_signal(
            barrier, inc=1, device_id={"tp": other * 2 + c}, device_id_type=MESH
        )
    krows = pl.ds(pl.multiple_of(c * 64, 64), 64)
    vrows = pl.ds(pl.multiple_of(128 + c * 64, 64), 64)
    orows = pl.ds(pl.multiple_of(c * 256, 256), 256)
    local = [
        pltpu.make_async_copy(wq_in, wq.at[c], lsem.at[0]),
        pltpu.make_async_copy(wk_in, wkv.at[krows], lsem.at[1]),
        pltpu.make_async_copy(wv_in, wkv.at[vrows], lsem.at[2]),
        pltpu.make_async_copy(wo_in, wo.at[orows], lsem.at[3]),
        pltpu.make_async_copy(small, sm.at[c], lsem.at[4]),
        pltpu.make_async_copy(
            wh_in.at[:, pl.ds(pl.multiple_of(chip * WIDE, WIDE), WIDE)],
            whp.at[c, chip],
            lsem.at[5],
        ),
    ]
    for copy in local:
        copy.start()
    k_ref[ROWS:, :] = jnp.zeros((LANES - ROWS, HS), BF16)
    v_ref[ROWS:, :] = jnp.zeros((LANES - ROWS, HS), BF16)
    hid[ROWS:, :] = jnp.zeros((LANES - ROWS, WIDE), BF16)
    pl.semaphore_wait(barrier, 8)

    sib = [
        send(SIB_X + r, x4.at[2 * (1 - c) + r], sib_x.at[r], sibling) for r in range(2)
    ]
    sib_w = [
        send(SIB_SMALL, small, sm.at[c], sibling),
        send(SIB_WQ, wq_in, wq.at[c], sibling),
        send(SIB_WK, wk_in, wkv.at[krows], sibling),
        send(SIB_WV, wv_in, wkv.at[vrows], sibling),
        send(SIB_WO, wo_in, wo.at[orows], sibling),
    ]

    ag = [[None] * 7 for _ in range(2)]
    rs = [[None] * 7 for _ in range(2)]
    near = {1: xp, -1: xm}
    way = (1, -1)

    for r in range(2):
        sib[r].wait_recv()
        mine, theirs = x4[2 * c + r], sib_x[r]
        left = jnp.where(c == 0, mine, theirs)
        right = jnp.where(c == 0, theirs, mine)
        xg[r, chip] = jnp.concatenate([left, right], axis=1)
        here = xg.at[r, chip]
        ag[r][0] = send(AG + 7 * r, here, here, core(xp, zh))
        ag[r][1] = send(AG + 7 * r + 1, here, here, core(xm, zh))
        ag[r][2] = send(AG + 7 * r + 2, here, here, core(x, zo))

    for r in range(2):
        w = way[r]
        base = AG + 7 * r
        ag[r][0].wait_recv()
        ag[r][1].wait_recv()
        part = xg.at[r, block(near[-w], zh)]
        ag[r][3] = send(base + 3, part, part, core(near[w], zh))
        ag[r][2].wait_recv()
        part = xg.at[r, block(x, zo)]
        ag[r][4] = send(base + 4, part, part, core(xp, zh))
        ag[r][5] = send(base + 5, part, part, core(xm, zh))
    head = [
        send(
            HEAD + d,
            wh_in.at[:, pl.ds(pl.multiple_of(other * WIDE, WIDE), WIDE)],
            whp.at[c, chip],
            {"tp": other * 2 + c},
        )
        for d, other in enumerate(others)
    ]
    for r in range(2):
        ag[r][3].wait_recv()
        part = xg.at[r, block(xx, zh)]
        ag[r][6] = send(AG + 7 * r + 6, part, part, core(x, zo))

    for copy in local:
        copy.wait()
    for copy in sib_w:
        copy.wait_recv()
    q_bias = [sm[p, 0:1, :] for p in range(2)]
    v_bias = sm[0, 1:2, 0:HS] + sm[1, 2:3, 0:HS]

    def project(xs, zs):
        columns = pl.ds(pl.multiple_of(block(xs, zs) * WIDE, WIDE), WIDE)
        return jnp.dot(ctx[...], wo[:, columns], preferred_element_type=F32)

    def attend(r):
        ag[r][4].wait_recv()
        ag[r][5].wait_recv()
        ag[r][6].wait_recv()

        def square(j, total):
            wide = xg[r, j].astype(F32)
            return total + jnp.sum(wide * wide, axis=1, keepdims=True)

        total = lax.fori_loop(0, CHIPS, square, jnp.zeros((ROWS, 1), F32))
        inverse = lax.rsqrt(total * (1.0 / D) + EPS)
        acc_q[...] = jnp.zeros_like(acc_q)
        acc_kv[...] = jnp.zeros_like(acc_kv)

        def lap(j, carry):
            gain = gains[0, pl.ds(j, 1), :]
            normed = (xg[r, j].astype(F32) * inverse * gain).astype(BF16)
            depth = pl.ds(pl.multiple_of(j * WIDE, WIDE), WIDE)
            for p in range(2):
                acc_q[p] += jnp.dot(normed, wq[p, depth, :], preferred_element_type=F32)
            acc_kv[...] += dot_nt(normed, wkv[:, depth])
            return carry

        lax.fori_loop(0, CHIPS, lap, 0)
        for p in range(2):
            q_ref[p] = (acc_q[p] + q_bias[p]).astype(BF16)
        k_ref[0:ROWS, :] = acc_kv[:, 0:HS].astype(BF16)
        v_ref[0:ROWS, :] = (acc_kv[:, HS:] + v_bias).astype(BF16)
        length = lengths[2 * c + r]
        valid = lax.broadcasted_iota(jnp.int32, (ROWS, LANES), 1) < length
        for n in range(4):
            at = slice((n % 2) * HS, (n % 2 + 1) * HS)
            scores = dot_nt(q_ref[n // 2, :, at], k_ref[...]) * HS ** (-0.5)
            scores = jnp.where(valid, scores, F32(-1e30))
            peak = jnp.max(scores, axis=1, keepdims=True)
            expo = jnp.exp(scores - peak)
            prob = (expo / jnp.sum(expo, axis=1, keepdims=True)).astype(BF16)
            ctx[:, n * HS : (n + 1) * HS] = jnp.dot(
                prob, v_ref[...], preferred_element_type=F32
            ).astype(BF16)

    def put(r, slot, value, target):
        stage[r, slot] = value.astype(BF16)
        rs[r][slot] = send(RS + 7 * r + slot, stage.at[r, slot], got.at[r, slot], target)

    def take(r, slot):
        rs[r][slot].wait_recv()
        return got[r, slot].astype(F32)

    for r in range(2):
        w = way[r]
        attend(r)
        put(r, 0, project(xx, zo), core(x, zo))
        put(r, 1, project(xp, zo), core(xp, zh))
        put(r, 2, project(xm, zo), core(xm, zh))
        put(r, 3, project(near[-w], zh), core(near[-w], zh))
        stage[r, 4] = project(xx, zh).astype(BF16)
        stage[r, 5] = project(x, zo).astype(BF16)
        stage[r, 6] = project(near[w], zh).astype(BF16)
        own = (project(x, zh)).astype(BF16)
        stage[r, 7] = own

    def staged(r, slot):
        return stage[r, slot].astype(F32)

    for r in range(2):
        put(r, 4, staged(r, 4) + take(r, 0), core(near[way[r]], zh))
        put(r, 5, staged(r, 5) + take(r, 1) + take(r, 2), core(x, zo))
    for r in range(2):
        put(r, 6, staged(r, 6) + take(r, 4), core(near[way[r]], zh))

    for copy in head:
        copy.wait_recv()
    sib_head = send(SIB_HEAD, whp.at[c], whp.at[c], sibling)
    sib_head.wait_recv()
    head_gain = gains[1, pl.ds(chip, 1), :]
    for p in range(2):
        raw = whp[p].reshape(CHIPS * 32, WIDE).astype(F32)
        whg[p] = (raw * head_gain).astype(BF16)

    sib_hid = []
    logit = [[], []]
    for r in range(2):
        summed = staged(r, 7) + take(r, 3) + take(r, 6) + take(r, 5)
        hidden = (xg[r, chip].astype(F32) + summed).astype(BF16)
        hid[0:ROWS, :] = hidden
        left, right = hidden[:, 0:HALF], hidden[:, HALF:]
        hid_out[2 * c + r] = jnp.where(c == 0, left, right)
        hid_send[r] = jnp.where(c == 0, right, left)
        sib_hid.append(
            send(SIB_HID + r, hid_send.at[r], hid_out.at[2 * c + r], sibling)
        )
        wide = hid[...].astype(F32)
        squares = jnp.sum(wide * wide, axis=1, keepdims=True)
        squares = jnp.broadcast_to(squares, (LANES, HS)).T[0:16]
        high = squares.astype(BF16).astype(F32)
        rest = squares - high
        mid = rest.astype(BF16).astype(F32)
        low = rest - mid
        row = lax.broadcasted_iota(jnp.int32, (16, LANES), 0)
        packed = jnp.where(
            row == 0, high, jnp.where(row == 1, mid, jnp.where(row == 2, low, 0.0))
        ).astype(BF16)
        for p in range(2):
            part = dot_nt(whg[p], hid[...]).astype(BF16)
            for i in range(CHIPS):
                lmsg[r, i, p * 32 : (p + 1) * 32, :] = part[i * 32 : (i + 1) * 32]
        for i in range(CHIPS):
            lmsg[r, i, 64:80, :] = packed
        for d, other in enumerate(others):
            logit[r].append(
                send(
                    LOGIT + 7 * r + d,
                    lmsg.at[r, other],
                    lgot.at[r, chip],
                    {"tp": other * 2 + c},
                )
            )
        lgot[r, chip] = lmsg[r, chip]

    logits = [None, None]
    stats = [[], []]
    for r in range(2):
        for copy in logit[r]:
            copy.wait_recv()
        total = lgot[r, 0].astype(F32)
        for i in range(1, CHIPS):
            total = total + lgot[r, i].astype(F32)
        squares = total[64:65] + total[65:66] + total[66:67]
        inverse = lax.rsqrt(squares * (1.0 / D) + EPS)
        logits[r] = total[0:64] * inverse
        top = jnp.max(logits[r], axis=0, keepdims=True)
        mass = jnp.sum(jnp.exp(logits[r] - top), axis=0, keepdims=True)
        row = lax.broadcasted_iota(jnp.int32, (8, LANES), 0)
        smsg[r] = jnp.where(row == 0, top, mass)
        for d, other in enumerate(others):
            stats[r].append(
                send(STAT + 7 * r + d, smsg.at[r], sgot.at[r, chip], {"tp": other * 2 + c})
            )
        sgot[r, chip] = smsg[r]

    sib_lp = []
    for r in range(2):
        for copy in stats[r]:
            copy.wait_recv()
        top = sgot[r, 0, 0:1, :]
        for i in range(1, CHIPS):
            top = jnp.maximum(top, sgot[r, i, 0:1, :])
        mass = jnp.zeros((1, LANES), F32)
        for i in range(CHIPS):
            mass = mass + sgot[r, i, 1:2, :] * jnp.exp(sgot[r, i, 0:1, :] - top)
        logprob = logits[r] - (top + jnp.log(mass))
        first, second = logprob[0:32], logprob[32:64]
        lp_out[2 * c + r] = jnp.where(c == 0, first, second)
        lp_send[r] = jnp.where(c == 0, second, first)
        sib_lp.append(send(SIB_LP + r, lp_send.at[r], lp_out.at[2 * c + r], sibling))
    for copy in sib_hid + sib_lp:
        copy.wait_recv()
    for copy in started:
        copy.wait_send()


def on_device(
    embeds,
    remask,
    lengths,
    mask_vec,
    attn_gain,
    w_query,
    q_bias,
    w_key,
    w_value,
    v_bias,
    w_out,
    head_gain,
    w_head,
):
    masked = jnp.where(remask[:, None] == 1, mask_vec[None, :], embeds)
    x4 = jnp.pad(masked.reshape(4, L, HALF), ((0, 0), (0, ROWS - L), (0, 0)))
    vb = v_bias.astype(F32)
    small = jnp.stack(
        [
            q_bias.astype(F32),
            jnp.pad(vb, (0, 192)),
            jnp.pad(vb, (64, 128)),
        ]
    )
    small = jnp.pad(small, ((0, 5), (0, 0)))
    gains = jnp.stack([attn_gain, head_gain]).astype(F32).reshape(2, CHIPS, WIDE)
    vmem = pl.BlockSpec(memory_space=pltpu.VMEM)
    anywhere = pl.BlockSpec(memory_space=pl.ANY)
    hid_out, lp_out = pl.pallas_call(
        kernel,
        out_shape=(
            jax.ShapeDtypeStruct((4, ROWS, HALF), BF16),
            jax.ShapeDtypeStruct((4, 32, LANES), F32),
        ),
        in_specs=[pl.BlockSpec(memory_space=pltpu.SMEM), vmem, vmem, vmem] + [anywhere] * 5,
        out_specs=(vmem, vmem),
        scratch_shapes=[
            pltpu.VMEM((2, ROWS, HALF), BF16),
            pltpu.VMEM((2, CHIPS, ROWS, WIDE), BF16),
            pltpu.VMEM((2, D, 256), BF16),
            pltpu.VMEM((256, D), BF16),
            pltpu.VMEM((512, D), BF16),
            pltpu.VMEM((2, CHIPS, 32, WIDE), BF16),
            pltpu.VMEM((2, CHIPS * 32, WIDE), BF16),
            pltpu.VMEM((2, 8, 256), F32),
            pltpu.VMEM((2, ROWS, 256), F32),
            pltpu.VMEM((ROWS, 256), F32),
            pltpu.VMEM((2, ROWS, 256), BF16),
            pltpu.VMEM((LANES, HS), BF16),
            pltpu.VMEM((LANES, HS), BF16),
            pltpu.VMEM((ROWS, 512), BF16),
            pltpu.VMEM((2, 8, ROWS, WIDE), BF16),
            pltpu.VMEM((2, 7, ROWS, WIDE), BF16),
            pltpu.VMEM((LANES, WIDE), BF16),
            pltpu.VMEM((2, ROWS, HALF), BF16),
            pltpu.VMEM((2, CHIPS, 80, LANES), BF16),
            pltpu.VMEM((2, CHIPS, 80, LANES), BF16),
            pltpu.VMEM((2, 8, LANES), F32),
            pltpu.VMEM((2, CHIPS, 8, LANES), F32),
            pltpu.VMEM((2, 32, LANES), F32),
            pltpu.SemaphoreType.DMA((COPIES,)),
            pltpu.SemaphoreType.DMA((COPIES,)),
            pltpu.SemaphoreType.DMA((6,)),
        ],
        compiler_params=pltpu.CompilerParams(
            collective_id=0, has_side_effects=True, vmem_limit_bytes=56 << 20
        ),
        name="refine",
    )(
        lengths,
        x4,
        small,
        gains,
        w_query,
        w_key.T,
        w_value.T,
        w_out,
        w_head.T,
    )
    hidden = hid_out[:, :L].reshape(4 * L, HALF)
    logprob = lp_out[:, :, :L].transpose(0, 2, 1).reshape(4 * L, 32)
    return hidden, logprob


def solution(mesh):
    placed = (
        P("rep", "tp"),
        P("rep"),
        P("rep"),
        P("tp"),
        P(),
        P(None, "tp"),
        P("tp"),
        P(None, "tp"),
        P(None, "tp"),
        P("tp"),
        P("tp", None),
        P(),
        P(None, "tp"),
    )
    return jax.shard_map(
        on_device,
        mesh=mesh,
        in_specs=placed,
        out_specs=(P("rep", "tp"), P("rep", "tp")),
        check_vma=False,
    )
```

time: 479 us -> 109 us (0.23)
  waiting for transfers between devices: 385 us -> 0 us
  Pallas kernels: 0 us -> 95.5 us
  other arithmetic: 30.8 us -> 3.77 us
  matrix products: 22.3 us -> 0 us
  local copies, waits for them, and re-layouts: 23.9 us -> 8.75 us
  between operations: 14.6 us -> 0.68 us
    all_gather x2 -> x0, waiting for transfers between devices: 153 us -> none  [the longest x1 77.8 us: on_device(): gathered = lax.all_gather(masked_local, 'tp', axis=1, tiled=True)]
    unnamed x5 -> x0, waiting for transfers between devices: 129 us -> none
    reduce_scatter x1 -> x0, waiting for transfers between devices: 102 us -> none  [on_device(): lax.psum_scatter(lax.dot_general(w_out, context, (((0,), (1,)), ((), ()))...]
    pallas_call x0 -> x1, Pallas kernels: none -> 95.5 us  [on_device(): pl.pallas_call(kernel, out_shape=(jax.ShapeDtypeStruct((4, ROWS, HALF), B...]
    dot_general x6 -> x0, matrix products: 19.4 us -> none  [the longest x1 5.38 us: on_device(): lax.dot_general(w_out, context, (((0,), (1,)), ((), ())), preferred_eleme...]
    unnamed x32 -> x1, local copies, waits for them, and re-layouts: 15.6 us -> 1.08 us
    convert_element_type x6 -> x1, other arithmetic: 13.5 us -> 0.62 us  [on_device(): jnp.stack([attn_gain, head_gain]).astype(F32).reshape(2, CHIPS, WIDE)]
    reduce_sum x3 -> x0, other arithmetic: 11.3 us -> none  [the longest x2 11.2 us: rms_norm(): inverse = lax.rsqrt(jnp.mean(wide * wide, axis=-1, keepdims=True) + EPS)]
  transfers between devices with their start and end apart: 6 -> 0, of which waited for: 4 -> 0; matrix products, arithmetic and copies ran while one was open for 2% -> 0% of each run, Pallas kernels for 0% -> 0%
where the time goes in v1:
time: 109 us
  Pallas kernels  95.5 us (88%)
  local copies, waits for them, and re-layouts  8.75 us (8%)
  other arithmetic  3.77 us (3%)
    pallas_call x1, Pallas kernels, on_device(): pl.pallas_call(kernel, out_shape=(jax.ShapeDtypeStruct((4, ROWS, HALF), B...  95.5 us

profile of v1, /device:TPU:1, one launch (start us, length us, event | category | flops | bytes accessed | tf_op | source)
XLA Modules:
  0.0 108.7 jit_solution(9361633454940477480)
XLA Ops:
  0.6 0.7 broadcast_compare_fusion
  1.3 0.7 stack.32
  2.0 0.8 fusion
  2.8 0.6 select_maximum_fusion.small
  3.4 0.7 stack.29
  4.1 0.7 stack.30
  4.9 0.6 maximum_convert_fusion.gains
  5.5 1.2 %broadcast_select_fusion = bf16[784,320]{0,1:T(8,128)(2,1)S(1)} fusion(bf16[784,320]{0,1:T(8,128)(2,1)} %param.13, pred[784]{0:T(1024)(128)(4,1)S(1)} %broadcast_compare_fusion, bf16[320]{0:T(512)(128)(2,1)} %param.16), kind=kLoop, calls=%fused_computation | loop fusion | flops 250880 | bytes 1004944 | tf_op jit(solution)/shard_map/jit(_where)/select_n | solution.py:374
  6.7 0.6 reshape.25
  7.2 0.9 copy.20
  8.1 0.9 pad.16.x4
  9.0 95.5 %refine.1 = (bf16[4,200,320]{2,1,0:T(8,128)(2,1)}, f32[4,32,256]{2,1,0:T(8,128)}) custom-call(s32[4]{0:T(128)} %lengths.1, bf16[4,200,320]{2,1,0:T(8,128)(2,1)} %pad.16.x4, f32[8,256]{1,0:T(8,128)} %select_maximum_fusion.small, f32[2,8,640]{2,1,0:T(8,128)} %maximum_convert_fusion.gains, bf16[5120,256]{1,0:T(8,128)(2,1)} %wq_in.1, bf16[64,5120]{1,0:T(8,128)(2,1)} %bitcast.13, ...), custom_call_target="tpu_custom_call" | custom-call | tf_op jit(solution)/shard_map/refine/pallas_call | solution.py:388
  104.5 1.3 %reshape.22 = bf16[784,320]{1,0:T(8,128)(2,1)S(1)} reshape(bf16[4,196,320]{2,1,0:T(8,128)(2,1)} %bitcast.15) | data formatting | bytes 1003520 | tf_op jit(solution)/shard_map/reshape | solution.py:439
  105.8 1.1 copy.19
  106.9 0.9 slice_bitcast_fusion
  107.8 0.1 copy.18
  107.9 0.8 reshape.23

commit v2 on v1

v2 whole, which is shorter than its diff:
```python
import jax
import jax.numpy as jnp
from jax import lax
from jax.experimental import pallas as pl
from jax.experimental.pallas import tpu as pltpu
from jax.sharding import PartitionSpec as P

HS = 128
L = 196
ROWS = 200
LANES = 256
CHIPS = 8
WIDE = 640
D = 5120
HALF = 320
TOKENS = 784
EPS = 1e-06
MESH = pl.DeviceIdType.MESH
F32 = jnp.float32
BF16 = jnp.bfloat16

SIB_X, SIB_WQ, SIB_WK, SIB_WV, SIB_WO, SIB_HEAD, SIB_QB, SIB_VB = 0, 2, 3, 4, 5, 6, 7, 8
AG = 9
RS = AG + 14
HEAD = RS + 14
LOGIT = HEAD + 7
STAT = LOGIT + 14
SIB_HID = STAT + 7
SIB_LP = SIB_HID + 2
COPIES = SIB_LP + 1


def dot_nt(a, b):
    return lax.dot_general(a, b, (((1,), (1,)), ((), ())), preferred_element_type=F32)


def lane_sums(wide):
    squares = wide * wide
    parts = squares[:, 0:128]
    for k in range(1, 5):
        parts = parts + squares[:, k * 128 : (k + 1) * 128]
    return jnp.sum(parts.T, axis=0, keepdims=True)


def kernel(
    lengths,
    embeds_in,
    remask_in,
    mask_vec_in,
    attn_gain_in,
    head_gain_in,
    qb_in,
    vb_in,
    wq_in,
    wk_in,
    wv_in,
    wo_in,
    wh_in,
    hid_out,
    lp_out,
    embeds,
    remask,
    mask_vec,
    attn_gain,
    head_gain,
    qb_mine,
    qb_theirs,
    vb_mine,
    vb_theirs,
    gains,
    masked,
    mine,
    sib_send,
    sib_x,
    xg,
    wq,
    wkv,
    wo,
    whp,
    whg,
    xn,
    ss,
    q_ref,
    k_ref,
    v_ref,
    ctx,
    kept,
    stage,
    got,
    hid,
    hid_send,
    hid_got,
    hid_mine,
    hid_all,
    lmsg,
    lgot,
    smsg,
    sgot,
    lp_send,
    lp_all,
    ssem,
    rsem,
    lsem,
):
    me = lax.axis_index("tp")
    x = me // 4
    zh = lax.rem(me // 2, 2)
    c = lax.rem(me, 2)
    chip = me // 2
    zo = 1 - zh
    xp, xm, xx = lax.rem(x + 1, 4), lax.rem(x + 3, 4), lax.rem(x + 2, 4)

    def core(xs, zs):
        return {"tp": xs * 4 + zs * 2 + c}

    def block(xs, zs):
        return xs * 2 + zs

    sibling = {"tp": me + 1 - 2 * c}
    others = [lax.rem(chip + d, CHIPS) for d in range(1, CHIPS)]
    started = []

    def send(number, src, dst, target):
        copy = pltpu.make_async_remote_copy(
            src_ref=src,
            dst_ref=dst,
            send_sem=ssem.at[number],
            recv_sem=rsem.at[number],
            device_id=target,
            device_id_type=MESH,
        )
        copy.start()
        started.append(copy)
        return copy

    barrier = pltpu.get_barrier_semaphore()
    for near_device in (sibling, core(xp, zh), core(xm, zh), core(x, zo)):
        pl.semaphore_signal(barrier, inc=1, device_id=near_device, device_id_type=MESH)
    krows = pl.ds(pl.multiple_of(c * 64, 64), 64)
    vrows = pl.ds(pl.multiple_of(128 + c * 64, 64), 64)
    orows = pl.ds(pl.multiple_of(c * 256, 256), 256)
    early = [
        pltpu.make_async_copy(embeds_in, embeds, lsem.at[0]),
        pltpu.make_async_copy(remask_in, remask, lsem.at[1]),
        pltpu.make_async_copy(mask_vec_in, mask_vec, lsem.at[2]),
    ]
    local = [
        pltpu.make_async_copy(attn_gain_in, attn_gain, lsem.at[3]),
        pltpu.make_async_copy(head_gain_in, head_gain, lsem.at[4]),
        pltpu.make_async_copy(qb_in, qb_mine, lsem.at[5]),
        pltpu.make_async_copy(vb_in, vb_mine, lsem.at[6]),
        pltpu.make_async_copy(wq_in, wq.at[c], lsem.at[7]),
        pltpu.make_async_copy(wk_in, wkv.at[krows], lsem.at[8]),
        pltpu.make_async_copy(wv_in, wkv.at[vrows], lsem.at[9]),
    ]
    later = [
        pltpu.make_async_copy(wo_in, wo.at[orows], lsem.at[10]),
        pltpu.make_async_copy(
            wh_in.at[:, pl.ds(pl.multiple_of(chip * WIDE, WIDE), WIDE)],
            whp.at[c, chip],
            lsem.at[11],
        ),
    ]
    for copy in early + local + later:
        copy.start()
    k_ref[ROWS:, :] = jnp.zeros((LANES - ROWS, HS), BF16)
    v_ref[ROWS:, :] = jnp.zeros((LANES - ROWS, HS), BF16)
    hid[ROWS:, :] = jnp.zeros((LANES - ROWS, WIDE), BF16)
    for copy in early:
        copy.wait()
    flags = remask[...][None, :]
    fill = jnp.broadcast_to(mask_vec[...].astype(F32)[None, :], (8, HALF)).T[:, 0:1]
    masked[TOKENS:, :] = jnp.zeros((8, HALF), F32)
    for k in range(7):
        at = slice(128 * k, min(128 * (k + 1), TOKENS))
        masked[at, :] = jnp.where(flags[:, at] == 1, fill, embeds[:, at].astype(F32)).T
    for r in range(2):
        low, high = masked[L * r : L * r + ROWS], masked[L * (r + 2) : L * (r + 2) + ROWS]
        mine[r] = jnp.where(c == 0, low, high)
        sib_send[r] = jnp.where(c == 0, high, low).astype(BF16)
    pl.semaphore_wait(barrier, 4)

    sib = [send(SIB_X + r, sib_send.at[r], sib_x.at[r], sibling) for r in range(2)]
    sib_w = [
        send(SIB_QB, qb_in, qb_theirs, sibling),
        send(SIB_VB, vb_in, vb_theirs, sibling),
        send(SIB_WQ, wq_in, wq.at[c], sibling),
        send(SIB_WK, wk_in, wkv.at[krows], sibling),
        send(SIB_WV, wv_in, wkv.at[vrows], sibling),
        send(SIB_WO, wo_in, wo.at[orows], sibling),
    ]

    ag = [[None] * 7 for _ in range(2)]
    rs = [[None] * 7 for _ in range(2)]
    near = {1: xp, -1: xm}
    way = (1, -1)

    def assemble(r):
        sib[r].wait_recv()
        theirs = sib_x[r].astype(F32)
        left = jnp.where(c == 0, mine[r], theirs)
        right = jnp.where(c == 0, theirs, mine[r])
        wide = jnp.concatenate([left, right], axis=1)
        xg[r, chip] = wide.astype(BF16)

    def gather(r, number, part, target):
        part = xg.at[r, part]
        ag[r][number] = send(AG + 7 * r + number, part, part, target)

    assemble(0)
    gather(0, 0, chip, core(xp, zh))
    gather(0, 1, chip, core(xm, zh))
    gather(0, 2, chip, core(x, zo))
    assemble(1)
    gather(1, 1, chip, core(xm, zh))
    gather(1, 2, chip, core(x, zo))

    def square(r, j, first=False):
        squares = xg[r, j].astype(F32)
        squares = squares * squares
        parts = squares[:, 0:128]
        for k in range(1, 5):
            parts = parts + squares[:, k * 128 : (k + 1) * 128]
        ss[r] = parts if first else ss[r] + parts

    def project(r, xs, zs):
        columns = pl.ds(pl.multiple_of(block(xs, zs) * WIDE, WIDE), WIDE)
        return jnp.dot(ctx[r], wo[:, columns], preferred_element_type=F32)

    def attend(r):
        total = jnp.sum(ss[r], axis=1, keepdims=True)
        inverse = lax.rsqrt(total * (1.0 / D) + EPS)
        for j in range(CHIPS):
            at = slice(j * WIDE, (j + 1) * WIDE)
            xn[:, at] = (xg[r, j].astype(F32) * inverse * gains[0:1, at]).astype(BF16)
        ours, theirs = qb_mine[...].astype(F32)[None, :], qb_theirs[...].astype(F32)[None, :]
        for p in range(2):
            bias = jnp.where(c == p, ours, theirs)
            q_ref[p] = (
                jnp.dot(xn[...], wq[p], preferred_element_type=F32) + bias
            ).astype(BF16)
        ours, theirs = vb_mine[...].astype(F32)[None, :], vb_theirs[...].astype(F32)[None, :]
        v_bias = jnp.concatenate(
            [jnp.where(c == 0, ours, theirs), jnp.where(c == 0, theirs, ours)], axis=1
        )
        key_value = dot_nt(xn[...], wkv[...])
        k_ref[0:ROWS, :] = key_value[:, 0:HS].astype(BF16)
        v_ref[0:ROWS, :] = (key_value[:, HS:] + v_bias).astype(BF16)
        length = lengths[2 * c + r]
        valid = lax.broadcasted_iota(jnp.int32, (ROWS, LANES), 1) < length
        for n in range(4):
            at = slice((n % 2) * HS, (n % 2 + 1) * HS)
            scores = dot_nt(q_ref[n // 2, :, at], k_ref[...]) * HS ** (-0.5)
            scores = jnp.where(valid, scores, F32(-1e30))
            peak = jnp.max(scores, axis=1, keepdims=True)
            expo = jnp.exp(scores - peak)
            prob = (expo / jnp.sum(expo, axis=1, keepdims=True)).astype(BF16)
            ctx[r, :, n * HS : (n + 1) * HS] = jnp.dot(
                prob, v_ref[...], preferred_element_type=F32
            ).astype(BF16)

    def put(r, slot, value, target):
        stage[r, slot] = value.astype(BF16)
        rs[r][slot] = send(RS + 7 * r + slot, stage.at[r, slot], got.at[r, slot], target)

    def take(r, slot):
        rs[r][slot].wait_recv()
        return got[r, slot].astype(F32)

    def first_sends(r):
        w = way[r]
        put(r, 0, project(r, xx, zo), core(x, zo))
        put(r, 1, project(r, xp, zo), core(xp, zh))
        put(r, 2, project(r, xm, zo), core(xm, zh))
        put(r, 3, project(r, near[-w], zh), core(near[-w], zh))

    def keep(r):
        kept[r, 0] = project(r, xx, zh)
        kept[r, 1] = project(r, x, zo)
        kept[r, 2] = project(r, near[way[r]], zh)
        kept[r, 3] = project(r, x, zh)

    square(0, chip, True)
    square(1, chip, True)
    ag[0][0].wait_recv()
    gather(0, 3, block(xm, zh), core(xp, zh))
    ag[0][2].wait_recv()
    gather(0, 4, block(x, zo), core(xp, zh))
    gather(0, 5, block(x, zo), core(xm, zh))
    gather(1, 0, chip, core(xp, zh))
    square(0, block(xm, zh))
    square(0, block(x, zo))
    ag[0][1].wait_recv()
    square(0, block(xp, zh))
    ag[1][1].wait_recv()
    gather(1, 3, block(xp, zh), core(xm, zh))
    ag[0][3].wait_recv()
    gather(0, 6, block(xx, zh), core(x, zo))
    ag[1][2].wait_recv()
    gather(1, 4, block(x, zo), core(xp, zh))
    gather(1, 5, block(x, zo), core(xm, zh))
    square(0, block(xx, zh))
    square(1, block(xp, zh))
    square(1, block(x, zo))
    for copy in local + later:
        copy.wait()
    for copy in sib_w:
        copy.wait_recv()
    gains[0:1, :] = attn_gain[...].astype(F32)[None, :]
    gains[1:2, :] = head_gain[...].astype(F32)[None, :]
    ag[0][5].wait_recv()
    square(0, block(xp, zo))
    ag[0][4].wait_recv()
    square(0, block(xm, zo))
    ag[0][6].wait_recv()
    square(0, block(xx, zo))
    attend(0)
    first_sends(0)
    ag[1][3].wait_recv()
    gather(1, 6, block(xx, zh), core(x, zo))
    head = [
        send(
            HEAD + d,
            wh_in.at[:, pl.ds(pl.multiple_of(other * WIDE, WIDE), WIDE)],
            whp.at[c, chip],
            {"tp": other * 2 + c},
        )
        for d, other in enumerate(others)
    ]
    keep(0)
    square(1, block(xx, zh))
    ag[1][0].wait_recv()
    square(1, block(xm, zh))
    ag[1][5].wait_recv()
    square(1, block(xp, zo))
    ag[1][4].wait_recv()
    square(1, block(xm, zo))
    ag[1][6].wait_recv()
    square(1, block(xx, zo))
    attend(1)
    first_sends(1)
    put(0, 4, kept[0, 0] + take(0, 0), core(near[way[0]], zh))
    keep(1)
    put(0, 5, kept[0, 1] + take(0, 1) + take(0, 2), core(x, zo))
    put(1, 4, kept[1, 0] + take(1, 0), core(near[way[1]], zh))
    put(0, 6, kept[0, 2] + take(0, 4), core(near[way[0]], zh))
    put(1, 5, kept[1, 1] + take(1, 1) + take(1, 2), core(x, zo))
    for copy in head:
        copy.wait_recv()
    sib_head = send(SIB_HEAD, whp.at[c], whp.at[c], sibling)
    put(1, 6, kept[1, 2] + take(1, 4), core(near[way[1]], zh))
    sib_head.wait_recv()
    gain = gains[1:2, pl.ds(pl.multiple_of(chip * WIDE, WIDE), WIDE)]
    for p in range(2):
        raw = whp[p].reshape(CHIPS * 32, WIDE).astype(F32)
        whg[p] = (raw * gain).astype(BF16)

    sib_hid = []
    logit = [[], []]
    for r in range(2):
        summed = kept[r, 3] + take(r, 3) + take(r, 6) + take(r, 5)
        hidden = (xg[r, chip].astype(F32) + summed).astype(BF16)
        hid[0:ROWS, :] = hidden
        for p in range(2):
            part = dot_nt(whg[p], hid[...]).astype(BF16)
            for i in range(CHIPS):
                lmsg[r, i, p * 32 : (p + 1) * 32, :] = part[i * 32 : (i + 1) * 32]
        squares = jnp.broadcast_to(lane_sums(hid[...].astype(F32)), (16, LANES))
        high = squares.astype(BF16).astype(F32)
        rest = squares - high
        mid = rest.astype(BF16).astype(F32)
        low = rest - mid
        row = lax.broadcasted_iota(jnp.int32, (16, LANES), 0)
        triple = jnp.where(
            row == 0, high, jnp.where(row == 1, mid, jnp.where(row == 2, low, 0.0))
        ).astype(BF16)
        for i in range(CHIPS):
            lmsg[r, i, 64:80, :] = triple
        for d, other in enumerate(others):
            logit[r].append(
                send(
                    LOGIT + 7 * r + d,
                    lmsg.at[r, other],
                    lgot.at[r, chip],
                    {"tp": other * 2 + c},
                )
            )
        lgot[r, chip] = lmsg[r, chip]
        left, right = hidden[:, 0:HALF], hidden[:, HALF:]
        hid_send[r] = jnp.where(c == 0, right, left)
        sib_hid.append(send(SIB_HID + r, hid_send.at[r], hid_got.at[r], sibling))
        hid_mine[r] = jnp.where(c == 0, left, right)

    for r in range(2):
        sib_hid[r].wait_recv()
        ours, theirs = hid_mine[r].astype(F32), hid_got[r].astype(F32)
        hid_all[L * r : L * (r + 1), :] = jnp.where(c == 0, ours, theirs)[0:L]
        hid_all[L * (r + 2) : L * (r + 3), :] = jnp.where(c == 0, theirs, ours)[0:L]
    for k in range(7):
        width = min(128, TOKENS - 128 * k)
        hid_out[:, 128 * k : 128 * k + width] = hid_all[128 * k : 128 * k + width, :].T.astype(
            BF16
        )

    logits = [None, None]
    smsg[...] = jnp.zeros_like(smsg)
    for r in range(2):
        for copy in logit[r]:
            copy.wait_recv()
        total = lgot[r, 0].astype(F32)
        for i in range(1, CHIPS):
            total = total + lgot[r, i].astype(F32)
        squares = total[64:65] + total[65:66] + total[66:67]
        inverse = lax.rsqrt(squares * (1.0 / D) + EPS)
        logits[r] = total[0:64] * inverse
        top = jnp.max(logits[r], axis=0, keepdims=True)
        smsg[2 * r : 2 * r + 1, :] = top
        smsg[2 * r + 1 : 2 * r + 2, :] = jnp.sum(
            jnp.exp(logits[r] - top), axis=0, keepdims=True
        )
    stats = [
        send(STAT + d, smsg, sgot.at[chip], {"tp": other * 2 + c})
        for d, other in enumerate(others)
    ]
    sgot[chip] = smsg[...]
    for copy in stats:
        copy.wait_recv()
    for r in range(2):
        tops = [sgot[i, 2 * r : 2 * r + 1, :] for i in range(CHIPS)]
        top = tops[0]
        for other_top in tops[1:]:
            top = jnp.maximum(top, other_top)
        mass = jnp.zeros((1, LANES), F32)
        for i in range(CHIPS):
            mass = mass + sgot[i, 2 * r + 1 : 2 * r + 2, :] * jnp.exp(tops[i] - top)
        logprob = logits[r] - (top + jnp.log(mass))
        first, second = logprob[0:32], logprob[32:64]
        lp_all[2 * c + r] = jnp.where(c == 0, first, second)
        lp_send[r] = jnp.where(c == 0, second, first)
    send(SIB_LP, lp_send, lp_all.at[pl.ds(2 * c, 2)], sibling).wait_recv()
    lp_out[...] = jnp.concatenate([lp_all[n, :, 0:L] for n in range(4)], axis=1)
    for copy in started:
        copy.wait_send()


def on_device(
    embeds,
    remask,
    lengths,
    mask_vec,
    attn_gain,
    w_query,
    q_bias,
    w_key,
    w_value,
    v_bias,
    w_out,
    head_gain,
    w_head,
):
    vmem = pl.BlockSpec(memory_space=pltpu.VMEM)
    anywhere = pl.BlockSpec(memory_space=pl.ANY)
    hidden, logprob = pl.pallas_call(
        kernel,
        out_shape=(
            jax.ShapeDtypeStruct((HALF, TOKENS), BF16),
            jax.ShapeDtypeStruct((32, TOKENS), F32),
        ),
        in_specs=[pl.BlockSpec(memory_space=pltpu.SMEM)] + [anywhere] * 12,
        out_specs=(vmem, vmem),
        scratch_shapes=[
            pltpu.VMEM((HALF, TOKENS), BF16),
            pltpu.VMEM((TOKENS,), jnp.int32),
            pltpu.VMEM((HALF,), BF16),
            pltpu.VMEM((D,), BF16),
            pltpu.VMEM((D,), BF16),
            pltpu.VMEM((256,), BF16),
            pltpu.VMEM((256,), BF16),
            pltpu.VMEM((64,), BF16),
            pltpu.VMEM((64,), BF16),
            pltpu.VMEM((8, D), F32),
            pltpu.VMEM((TOKENS + 8, HALF), F32),
            pltpu.VMEM((2, ROWS, HALF), F32),
            pltpu.VMEM((2, ROWS, HALF), BF16),
            pltpu.VMEM((2, ROWS, HALF), BF16),
            pltpu.VMEM((2, CHIPS, ROWS, WIDE), BF16),
            pltpu.VMEM((2, D, 256), BF16),
            pltpu.VMEM((256, D), BF16),
            pltpu.VMEM((512, D), BF16),
            pltpu.VMEM((2, CHIPS, 32, WIDE), BF16),
            pltpu.VMEM((2, CHIPS * 32, WIDE), BF16),
            pltpu.VMEM((ROWS, D), BF16),
            pltpu.VMEM((2, ROWS, 128), F32),
            pltpu.VMEM((2, ROWS, 256), BF16),
            pltpu.VMEM((LANES, HS), BF16),
            pltpu.VMEM((LANES, HS), BF16),
            pltpu.VMEM((2, ROWS, 512), BF16),
            pltpu.VMEM((2, 4, ROWS, WIDE), F32),
            pltpu.VMEM((2, 7, ROWS, WIDE), BF16),
            pltpu.VMEM((2, 7, ROWS, WIDE), BF16),
            pltpu.VMEM((LANES, WIDE), BF16),
            pltpu.VMEM((2, ROWS, HALF), BF16),
            pltpu.VMEM((2, ROWS, HALF), BF16),
            pltpu.VMEM((2, ROWS, HALF), BF16),
            pltpu.VMEM((TOKENS, HALF), F32),
            pltpu.VMEM((2, CHIPS, 80, LANES), BF16),
            pltpu.VMEM((2, CHIPS, 80, LANES), BF16),
            pltpu.VMEM((8, LANES), F32),
            pltpu.VMEM((CHIPS, 8, LANES), F32),
            pltpu.VMEM((2, 32, LANES), F32),
            pltpu.VMEM((4, 32, LANES), F32),
            pltpu.SemaphoreType.DMA((COPIES,)),
            pltpu.SemaphoreType.DMA((COPIES,)),
            pltpu.SemaphoreType.DMA((12,)),
        ],
        compiler_params=pltpu.CompilerParams(
            collective_id=0, has_side_effects=True, vmem_limit_bytes=56 << 20
        ),
        name="refine",
    )(
        lengths,
        embeds.T,
        remask,
        mask_vec,
        attn_gain,
        head_gain,
        q_bias,
        v_bias,
        w_query,
        w_key.T,
        w_value.T,
        w_out,
        w_head.T,
    )
    return hidden.T, logprob.T


def solution(mesh):
    placed = (
        P("rep", "tp"),
        P("rep"),
        P("rep"),
        P("tp"),
        P(),
        P(None, "tp"),
        P("tp"),
        P(None, "tp"),
        P(None, "tp"),
        P("tp"),
        P("tp", None),
        P(),
        P(None, "tp"),
    )
    return jax.shard_map(
        on_device,
        mesh=mesh,
        in_specs=placed,
        out_specs=(P("rep", "tp"), P("rep", "tp")),
        check_vma=False,
    )
```

time: 109 us -> 103 us (0.945)
  local copies, waits for them, and re-layouts: 8.75 us -> 3.47 us
  other arithmetic: 3.77 us -> 0 us
  Pallas kernels: 95.5 us -> 98.6 us
    reshape x4 -> x0, local copies, waits for them, and re-layouts: 3.52 us -> none  [the longest x2 1.45 us: on_device(): x4 = jnp.pad(masked.reshape(4, L, HALF), ((0, 0), (0, ROWS - L), (0, 0)))]
    pallas_call x1, Pallas kernels: 95.5 us -> 98.6 us  [on_device(): pl.pallas_call(kernel, out_shape=(jax.ShapeDtypeStruct((HALF, TOKENS), BF...]
    unnamed x1 -> x2, local copies, waits for them, and re-layouts: 1.08 us -> 3.47 us
    pad x2 -> x0, local copies, waits for them, and re-layouts: 1.7 us -> none  [the longest x1 0.9 us: on_device(): x4 = jnp.pad(masked.reshape(4, L, HALF), ((0, 0), (0, ROWS - L), (0, 0)))]
    another operation x2 -> x0, local copies, waits for them, and re-layouts: 1.46 us -> none  [on_device(): jnp.stack([attn_gain, head_gain]).astype(F32).reshape(2, CHIPS, WIDE)]
    another operation x2 -> x0, other arithmetic: 1.26 us -> none  [on_device(): jnp.stack([q_bias.astype(F32), jnp.pad(vb, (0, 192)), jnp.pad(vb, (64, 12...]
    select_n x1 -> x0, other arithmetic: 1.19 us -> none  [on_device(): masked = jnp.where(remask[:, None] == 1, mask_vec[None, :], embeds)]
where the time goes in v2:
time: 103 us
  Pallas kernels  98.6 us (96%)
  local copies, waits for them, and re-layouts  3.47 us (3%)
    pallas_call x1, Pallas kernels, on_device(): pl.pallas_call(kernel, out_shape=(jax.ShapeDtypeStruct((HALF, TOKENS), BF...  98.6 us
    unnamed x2, local copies, waits for them, and re-layouts  3.47 us

profile of v2, /device:TPU:1, one launch (start us, length us, event | category | flops | bytes accessed | tf_op | source)
XLA Modules:
  0.0 102.7 jit_solution(2292810901102660436)
XLA Ops:
  0.6 98.6 %refine.1 = (bf16[320,784]{1,0:T(8,128)(2,1)}, f32[32,784]{1,0:T(8,128)}) custom-call(s32[4]{0:T(128)} %lengths.1, bf16[320,784]{1,0:T(8,128)(2,1)} %bitcast.8, s32[784]{0:T(1024)} %remask_in.1, bf16[320]{0:T(512)(128)(2,1)} %mask_vec_in.1, bf16[5120]{0:T(1024)(128)(2,1)} %attn_gain_in.1, bf16[5120]{0:T(1024)(128)(2,1)} %head_gain_in.1, ...), custom_call_target="tpu_custom_call" | custom-call | tf_op jit(solution)/shard_map/refine/pallas_call | solution.py:463
  99.2 1.9 %copy.17 = bf16[784,320]{0,1:T(8,128)(2,1)} copy(bf16[784,320]{0,1:T(8,128)(2,1)} %bitcast.9) | data formatting | bytes 1003520
  101.1 1.6 %copy.18 = f32[784,32]{0,1:T(8,128)} copy(f32[784,32]{0,1:T(8,128)} %bitcast.11) | data formatting | bytes 200704

commit v3 on v2

--- a/solution.py
+++ b/solution.py
@@ -134,8 +134,11 @@
         return copy
 
     barrier = pltpu.get_barrier_semaphore()
-    for near_device in (sibling, core(xp, zh), core(xm, zh), core(x, zo)):
-        pl.semaphore_signal(barrier, inc=1, device_id=near_device, device_id_type=MESH)
+    pl.semaphore_signal(barrier, inc=1, device_id=sibling, device_id_type=MESH)
+    for other in others:
+        pl.semaphore_signal(
+            barrier, inc=1, device_id={"tp": other * 2 + c}, device_id_type=MESH
+        )
     krows = pl.ds(pl.multiple_of(c * 64, 64), 64)
     vrows = pl.ds(pl.multiple_of(128 + c * 64, 64), 64)
     orows = pl.ds(pl.multiple_of(c * 256, 256), 256)
@@ -161,13 +164,15 @@
             lsem.at[11],
         ),
     ]
-    for copy in early + local + later:
+    for copy in early:
         copy.start()
     k_ref[ROWS:, :] = jnp.zeros((LANES - ROWS, HS), BF16)
     v_ref[ROWS:, :] = jnp.zeros((LANES - ROWS, HS), BF16)
     hid[ROWS:, :] = jnp.zeros((LANES - ROWS, WIDE), BF16)
     for copy in early:
         copy.wait()
+    for copy in local + later:
+        copy.start()
     flags = remask[...][None, :]
     fill = jnp.broadcast_to(mask_vec[...].astype(F32)[None, :], (8, HALF)).T[:, 0:1]
     masked[TOKENS:, :] = jnp.zeros((8, HALF), F32)
@@ -176,11 +181,19 @@
         masked[at, :] = jnp.where(flags[:, at] == 1, fill, embeds[:, at].astype(F32)).T
     for r in range(2):
         low, high = masked[L * r : L * r + ROWS], masked[L * (r + 2) : L * (r + 2) + ROWS]
-        mine[r] = jnp.where(c == 0, low, high)
         sib_send[r] = jnp.where(c == 0, high, low).astype(BF16)
-    pl.semaphore_wait(barrier, 4)
+    pl.semaphore_wait(barrier, CHIPS)
 
     sib = [send(SIB_X + r, sib_send.at[r], sib_x.at[r], sibling) for r in range(2)]
+    head = [
+        send(
+            HEAD + d,
+            wh_in.at[:, pl.ds(pl.multiple_of(other * WIDE, WIDE), WIDE)],
+            whp.at[c, chip],
+            {"tp": other * 2 + c},
+        )
+        for d, other in enumerate(others)
+    ]
     sib_w = [
         send(SIB_QB, qb_in, qb_theirs, sibling),
         send(SIB_VB, vb_in, vb_theirs, sibling),
@@ -194,6 +207,10 @@
     rs = [[None] * 7 for _ in range(2)]
     near = {1: xp, -1: xm}
     way = (1, -1)
+
+    for r in range(2):
+        low, high = masked[L * r : L * r + ROWS], masked[L * (r + 2) : L * (r + 2) + ROWS]
+        mine[r] = jnp.where(c == 0, low, high)
 
     def assemble(r):
         sib[r].wait_recv()
@@ -308,6 +325,9 @@
         copy.wait_recv()
     gains[0:1, :] = attn_gain[...].astype(F32)[None, :]
     gains[1:2, :] = head_gain[...].astype(F32)[None, :]
+    for copy in head:
+        copy.wait_recv()
+    sib_head = send(SIB_HEAD, whp.at[c], whp.at[c], sibling)
     ag[0][5].wait_recv()
     square(0, block(xp, zo))
     ag[0][4].wait_recv()
@@ -318,16 +338,13 @@
     first_sends(0)
     ag[1][3].wait_recv()
     gather(1, 6, block(xx, zh), core(x, zo))
-    head = [
-        send(
-            HEAD + d,
-            wh_in.at[:, pl.ds(pl.multiple_of(other * WIDE, WIDE), WIDE)],
-            whp.at[c, chip],
-            {"tp": other * 2 + c},
-        )
-        for d, other in enumerate(others)
-    ]
     keep(0)
+    sib_head.wait_recv()
+    gain = gains[1:2, pl.ds(pl.multiple_of(chip * WIDE, WIDE), WIDE)]
+    for p in range(2):
+        raw = whp[p].reshape(CHIPS * 32, WIDE).astype(F32)
+        whg[p] = (raw * gain).astype(BF16)
+
     square(1, block(xx, zh))
     ag[1][0].wait_recv()
     square(1, block(xm, zh))
@@ -337,24 +354,15 @@
     square(1, block(xm, zo))
     ag[1][6].wait_recv()
     square(1, block(xx, zo))
+    put(0, 4, kept[0, 0] + take(0, 0), core(near[way[0]], zh))
     attend(1)
     first_sends(1)
-    put(0, 4, kept[0, 0] + take(0, 0), core(near[way[0]], zh))
     keep(1)
     put(0, 5, kept[0, 1] + take(0, 1) + take(0, 2), core(x, zo))
     put(1, 4, kept[1, 0] + take(1, 0), core(near[way[1]], zh))
     put(0, 6, kept[0, 2] + take(0, 4), core(near[way[0]], zh))
     put(1, 5, kept[1, 1] + take(1, 1) + take(1, 2), core(x, zo))
-    for copy in head:
-        copy.wait_recv()
-    sib_head = send(SIB_HEAD, whp.at[c], whp.at[c], sibling)
     put(1, 6, kept[1, 2] + take(1, 4), core(near[way[1]], zh))
-    sib_head.wait_recv()
-    gain = gains[1:2, pl.ds(pl.multiple_of(chip * WIDE, WIDE), WIDE)]
-    for p in range(2):
-        raw = whp[p].reshape(CHIPS * 32, WIDE).astype(F32)
-        whg[p] = (raw * gain).astype(BF16)
-
     sib_hid = []
     logit = [[], []]
     for r in range(2):

time: 103 us -> 97.8 us (0.950)
  Pallas kernels: 98.6 us -> 93.5 us
    pallas_call x1, Pallas kernels: 98.6 us -> 93.5 us  [on_device(): pl.pallas_call(kernel, out_shape=(jax.ShapeDtypeStruct((HALF, TOKENS), BF...]
where the time goes in v3:
time: 97.8 us; the launch traced here: 97.6 us
  Pallas kernels  93.5 us (96%)
  local copies, waits for them, and re-layouts  3.47 us (4%)
    pallas_call x1, Pallas kernels, on_device(): pl.pallas_call(kernel, out_shape=(jax.ShapeDtypeStruct((HALF, TOKENS), BF...  93.5 us
    unnamed x2, local copies, waits for them, and re-layouts  3.47 us

profile of v3, /device:TPU:1, one launch (start us, length us, event | category | flops | bytes accessed | tf_op | source)
XLA Modules:
  0.0 97.6 jit_solution(9089097172746254403)
XLA Ops:
  0.6 93.5 %refine.1 = (bf16[320,784]{1,0:T(8,128)(2,1)}, f32[32,784]{1,0:T(8,128)}) custom-call(s32[4]{0:T(128)} %lengths.1, bf16[320,784]{1,0:T(8,128)(2,1)} %bitcast.8, s32[784]{0:T(1024)} %remask_in.1, bf16[320]{0:T(512)(128)(2,1)} %mask_vec_in.1, bf16[5120]{0:T(1024)(128)(2,1)} %attn_gain_in.1, bf16[5120]{0:T(1024)(128)(2,1)} %head_gain_in.1, ...), custom_call_target="tpu_custom_call" | custom-call | tf_op jit(solution)/shard_map/refine/pallas_call | solution.py:471
  94.1 1.9 %copy.17 = bf16[784,320]{0,1:T(8,128)(2,1)} copy(bf16[784,320]{0,1:T(8,128)(2,1)} %bitcast.9) | data formatting | bytes 1003520
  96.1 1.6 %copy.18 = f32[784,32]{0,1:T(8,128)} copy(f32[784,32]{0,1:T(8,128)} %bitcast.11) | data formatting | bytes 200704

commit v4 on v2

--- a/solution.py
+++ b/solution.py
@@ -25,9 +25,11 @@
 HEAD = RS + 14
 LOGIT = HEAD + 7
 STAT = LOGIT + 14
-SIB_HID = STAT + 7
+SIB_HID = STAT + 15
 SIB_LP = SIB_HID + 2
-COPIES = SIB_LP + 1
+PARTS = SIB_LP + 1
+COPIES = PARTS + 12
+PART_ROWS = (slice(0, 96), slice(96, ROWS))
 
 
 def dot_nt(a, b):
@@ -97,7 +99,7 @@
     smsg,
     sgot,
     lp_send,
-    lp_all,
+    lp_got,
     ssem,
     rsem,
     lsem,
@@ -134,8 +136,9 @@
         return copy
 
     barrier = pltpu.get_barrier_semaphore()
-    for near_device in (sibling, core(xp, zh), core(xm, zh), core(x, zo)):
-        pl.semaphore_signal(barrier, inc=1, device_id=near_device, device_id_type=MESH)
+    pl.semaphore_signal(barrier, inc=1, device_id=sibling, device_id_type=MESH)
+    for nd in (core(xp, zh), core(xm, zh), core(x, zo)):
+        pl.semaphore_signal(barrier, inc=1, device_id=nd, device_id_type=MESH)
     krows = pl.ds(pl.multiple_of(c * 64, 64), 64)
     vrows = pl.ds(pl.multiple_of(128 + c * 64, 64), 64)
     orows = pl.ds(pl.multiple_of(c * 256, 256), 256)
@@ -161,26 +164,38 @@
             lsem.at[11],
         ),
     ]
-    for copy in early + local + later:
+    for copy in early:
         copy.start()
     k_ref[ROWS:, :] = jnp.zeros((LANES - ROWS, HS), BF16)
     v_ref[ROWS:, :] = jnp.zeros((LANES - ROWS, HS), BF16)
     hid[ROWS:, :] = jnp.zeros((LANES - ROWS, WIDE), BF16)
     for copy in early:
         copy.wait()
+    for copy in local + later:
+        copy.start()
     flags = remask[...][None, :]
     fill = jnp.broadcast_to(mask_vec[...].astype(F32)[None, :], (8, HALF)).T[:, 0:1]
     masked[TOKENS:, :] = jnp.zeros((8, HALF), F32)
-    for k in range(7):
-        at = slice(128 * k, min(128 * (k + 1), TOKENS))
-        masked[at, :] = jnp.where(flags[:, at] == 1, fill, embeds[:, at].astype(F32)).T
-    for r in range(2):
+
+    def prepare(tiles, r):
+        for k in tiles:
+            at = slice(128 * k, min(128 * (k + 1), TOKENS))
+            tile = jnp.where(flags[:, at] == 1, fill, embeds[:, at].astype(F32))
+            masked[at, :] = tile.T
+        low, high = masked[L * r : L * r + ROWS], masked[L * (r + 2) : L * (r + 2) + ROWS]
+        sib_send[r] = jnp.where(c == 0, high, low).astype(BF16)
+
+    def pick(r):
         low, high = masked[L * r : L * r + ROWS], masked[L * (r + 2) : L * (r + 2) + ROWS]
         mine[r] = jnp.where(c == 0, low, high)
-        sib_send[r] = jnp.where(c == 0, high, low).astype(BF16)
+
+    prepare((0, 1, 3, 4), 0)
     pl.semaphore_wait(barrier, 4)
 
-    sib = [send(SIB_X + r, sib_send.at[r], sib_x.at[r], sibling) for r in range(2)]
+    sib = [send(SIB_X, sib_send.at[0], sib_x.at[0], sibling)]
+    pick(0)
+    prepare((2, 5, 6), 1)
+    sib.append(send(SIB_X + 1, sib_send.at[1], sib_x.at[1], sibling))
     sib_w = [
         send(SIB_QB, qb_in, qb_theirs, sibling),
         send(SIB_VB, vb_in, vb_theirs, sibling),
@@ -192,6 +207,7 @@
 
     ag = [[None] * 7 for _ in range(2)]
     rs = [[None] * 7 for _ in range(2)]
+    rs_part = {}
     near = {1: xp, -1: xm}
     way = (1, -1)
 
@@ -211,6 +227,7 @@
     gather(0, 0, chip, core(xp, zh))
     gather(0, 1, chip, core(xm, zh))
     gather(0, 2, chip, core(x, zo))
+    pick(1)
     assemble(1)
     gather(1, 1, chip, core(xm, zh))
     gather(1, 2, chip, core(x, zo))
@@ -263,16 +280,36 @@
         stage[r, slot] = value.astype(BF16)
         rs[r][slot] = send(RS + 7 * r + slot, stage.at[r, slot], got.at[r, slot], target)
 
+    def put_part(r, slot, n, value, target):
+        at = PART_ROWS[n]
+        stage[r, slot, at] = value.astype(BF16)
+        number = PARTS + 6 * r + (0, 0, 0, 0, 2, 0, 4)[slot] + n
+        src, dst = stage.at[r, slot, at], got.at[r, slot, at]
+        rs_part[r, slot, n] = send(number, src, dst, target)
+
+    def relay(r, slot, own, source, target):
+        for n, at in enumerate(PART_ROWS):
+            rs_part[r, source, n].wait_recv()
+            value = kept[r, own, at] + got[r, source, at].astype(F32)
+            put_part(r, slot, n, value, target)
+
     def take(r, slot):
-        rs[r][slot].wait_recv()
+        if slot == 6:
+            for n in range(2):
+                rs_part[r, slot, n].wait_recv()
+        else:
+            rs[r][slot].wait_recv()
         return got[r, slot].astype(F32)
 
     def first_sends(r):
         w = way[r]
-        put(r, 0, project(r, xx, zo), core(x, zo))
+        value = project(r, xx, zo)
+        for n, at in enumerate(PART_ROWS):
+            put_part(r, 0, n, value[at], core(x, zo))
         put(r, 1, project(r, xp, zo), core(xp, zh))
         put(r, 2, project(r, xm, zo), core(xm, zh))
-        put(r, 3, project(r, near[-w], zh), core(near[-w], zh))
+        if r == 0:
+            put(r, 3, project(r, near[-w], zh), core(near[-w], zh))
 
     def keep(r):
         kept[r, 0] = project(r, xx, zh)
@@ -337,18 +374,19 @@
     square(1, block(xm, zo))
     ag[1][6].wait_recv()
     square(1, block(xx, zo))
+    relay(0, 4, 0, 0, core(near[way[0]], zh))
     attend(1)
     first_sends(1)
-    put(0, 4, kept[0, 0] + take(0, 0), core(near[way[0]], zh))
     keep(1)
     put(0, 5, kept[0, 1] + take(0, 1) + take(0, 2), core(x, zo))
-    put(1, 4, kept[1, 0] + take(1, 0), core(near[way[1]], zh))
-    put(0, 6, kept[0, 2] + take(0, 4), core(near[way[0]], zh))
+    relay(1, 4, 0, 0, core(near[way[1]], zh))
+    relay(0, 6, 2, 4, core(near[way[0]], zh))
+    put(1, 3, project(1, near[-way[1]], zh), core(near[-way[1]], zh))
     put(1, 5, kept[1, 1] + take(1, 1) + take(1, 2), core(x, zo))
     for copy in head:
         copy.wait_recv()
     sib_head = send(SIB_HEAD, whp.at[c], whp.at[c], sibling)
-    put(1, 6, kept[1, 2] + take(1, 4), core(near[way[1]], zh))
+    relay(1, 6, 2, 4, core(near[way[1]], zh))
     sib_head.wait_recv()
     gain = gains[1:2, pl.ds(pl.multiple_of(chip * WIDE, WIDE), WIDE)]
     for p in range(2):
@@ -418,27 +456,34 @@
         smsg[2 * r + 1 : 2 * r + 2, :] = jnp.sum(
             jnp.exp(logits[r] - top), axis=0, keepdims=True
         )
-    stats = [
-        send(STAT + d, smsg, sgot.at[chip], {"tp": other * 2 + c})
-        for d, other in enumerate(others)
-    ]
-    sgot[chip] = smsg[...]
+    stats = []
+    for d, other in enumerate(others):
+        for k in range(2):
+            target = {"tp": other * 2 + (c if k == 0 else 1 - c)}
+            stats.append(send(STAT + 2 * d + k, smsg, sgot.at[c, chip], target))
+    stats.append(send(STAT + 14, smsg, sgot.at[c, chip], sibling))
+    sgot[c, chip] = smsg[...]
+    for r in range(2):
+        lp_send[r] = jnp.where(c == 0, logits[r][32:64], logits[r][0:32])
+    sib_lp = send(SIB_LP, lp_send, lp_got, sibling)
     for copy in stats:
         copy.wait_recv()
-    for r in range(2):
-        tops = [sgot[i, 2 * r : 2 * r + 1, :] for i in range(CHIPS)]
+    sib_lp.wait_recv()
+    pieces = []
+    for n in range(4):
+        plane, r = n // 2, n % 2
+        tops = [sgot[plane, i, 2 * r : 2 * r + 1, :] for i in range(CHIPS)]
         top = tops[0]
         for other_top in tops[1:]:
             top = jnp.maximum(top, other_top)
         mass = jnp.zeros((1, LANES), F32)
         for i in range(CHIPS):
-            mass = mass + sgot[i, 2 * r + 1 : 2 * r + 2, :] * jnp.exp(tops[i] - top)
-        logprob = logits[r] - (top + jnp.log(mass))
-        first, second = logprob[0:32], logprob[32:64]
-        lp_all[2 * c + r] = jnp.where(c == 0, first, second)
-        lp_send[r] = jnp.where(c == 0, second, first)
-    send(SIB_LP, lp_send, lp_all.at[pl.ds(2 * c, 2)], sibling).wait_recv()
-    lp_out[...] = jnp.concatenate([lp_all[n, :, 0:L] for n in range(4)], axis=1)
+            share = sgot[plane, i, 2 * r + 1 : 2 * r + 2, :]
+            mass = mass + share * jnp.exp(tops[i] - top)
+        ours = jnp.where(c == 0, logits[r][0:32], logits[r][32:64])
+        piece = jnp.where(c == plane, ours, lp_got[r]) - (top + jnp.log(mass))
+        pieces.append(piece[:, 0:L])
+    lp_out[...] = jnp.concatenate(pieces, axis=1)
     for copy in started:
         copy.wait_send()
 
@@ -506,9 +551,9 @@
             pltpu.VMEM((2, CHIPS, 80, LANES), BF16),
             pltpu.VMEM((2, CHIPS, 80, LANES), BF16),
             pltpu.VMEM((8, LANES), F32),
-            pltpu.VMEM((CHIPS, 8, LANES), F32),
+            pltpu.VMEM((2, CHIPS, 8, LANES), F32),
             pltpu.VMEM((2, 32, LANES), F32),
-            pltpu.VMEM((4, 32, LANES), F32),
+            pltpu.VMEM((2, 32, LANES), F32),
             pltpu.SemaphoreType.DMA((COPIES,)),
             pltpu.SemaphoreType.DMA((COPIES,)),
             pltpu.SemaphoreType.DMA((12,)),

time: 103 us -> 95.5 us (0.927)
  Pallas kernels: 98.6 us -> 91.2 us
    pallas_call x1, Pallas kernels: 98.6 us -> 91.2 us  [on_device(): pl.pallas_call(kernel, out_shape=(jax.ShapeDtypeStruct((HALF, TOKENS), BF...]
where the time goes in v4:
time: 95.5 us; the launch traced here: 95.3 us
  Pallas kernels  91.2 us (95%)
  local copies, waits for them, and re-layouts  3.47 us (4%)
    pallas_call x1, Pallas kernels, on_device(): pl.pallas_call(kernel, out_shape=(jax.ShapeDtypeStruct((HALF, TOKENS), BF...  91.2 us
    unnamed x2, local copies, waits for them, and re-layouts  3.47 us

profile of v4, /device:TPU:1, one launch (start us, length us, event | category | flops | bytes accessed | tf_op | source)
XLA Modules:
  0.0 95.3 jit_solution(563621971528601613)
XLA Ops:
  0.6 91.2 %refine.1 = (bf16[320,784]{1,0:T(8,128)(2,1)}, f32[32,784]{1,0:T(8,128)}) custom-call(s32[4]{0:T(128)} %lengths.1, bf16[320,784]{1,0:T(8,128)(2,1)} %bitcast.8, s32[784]{0:T(1024)} %remask_in.1, bf16[320]{0:T(512)(128)(2,1)} %mask_vec_in.1, bf16[5120]{0:T(1024)(128)(2,1)} %attn_gain_in.1, bf16[5120]{0:T(1024)(128)(2,1)} %head_gain_in.1, ...), custom_call_target="tpu_custom_call" | custom-call | tf_op jit(solution)/shard_map/refine/pallas_call | solution.py:508
  91.8 1.9 %copy.17 = bf16[784,320]{0,1:T(8,128)(2,1)} copy(bf16[784,320]{0,1:T(8,128)(2,1)} %bitcast.9) | data formatting | bytes 1003520
  93.8 1.6 %copy.18 = f32[784,32]{0,1:T(8,128)} copy(f32[784,32]{0,1:T(8,128)} %bitcast.11) | data formatting | bytes 200704

commit v5 on v4

--- a/solution.py
+++ b/solution.py
@@ -119,7 +119,7 @@
         return xs * 2 + zs
 
     sibling = {"tp": me + 1 - 2 * c}
-    others = [lax.rem(chip + d, CHIPS) for d in range(1, CHIPS)]
+    others = [lax.rem(chip + d, CHIPS) for d in (5, 3, 4, 1, 7, 2, 6)]
     started = []
 
     def send(number, src, dst, target):

time: 95.5 us -> 94.5 us (0.990)
  Pallas kernels: 91.2 us -> 90.2 us
    pallas_call x1, Pallas kernels: 91.2 us -> 90.2 us  [on_device(): pl.pallas_call(kernel, out_shape=(jax.ShapeDtypeStruct((HALF, TOKENS), BF...]
where the time goes in v5:
time: 94.5 us; the launch traced here: 94.3 us
  Pallas kernels  90.2 us (95%)
  local copies, waits for them, and re-layouts  3.47 us (4%)
    pallas_call x1, Pallas kernels, on_device(): pl.pallas_call(kernel, out_shape=(jax.ShapeDtypeStruct((HALF, TOKENS), BF...  90.2 us
    unnamed x2, local copies, waits for them, and re-layouts  3.47 us

profile of v5, /device:TPU:1, one launch (start us, length us, event | category | flops | bytes accessed | tf_op | source)
XLA Modules:
  0.0 94.3 jit_solution(10948985271625270950)
XLA Ops:
  0.6 90.2 %refine.1 = (bf16[320,784]{1,0:T(8,128)(2,1)}, f32[32,784]{1,0:T(8,128)}) custom-call(s32[4]{0:T(128)} %lengths.1, bf16[320,784]{1,0:T(8,128)(2,1)} %bitcast.8, s32[784]{0:T(1024)} %remask_in.1, bf16[320]{0:T(512)(128)(2,1)} %mask_vec_in.1, bf16[5120]{0:T(1024)(128)(2,1)} %attn_gain_in.1, bf16[5120]{0:T(1024)(128)(2,1)} %head_gain_in.1, ...), custom_call_target="tpu_custom_call" | custom-call | tf_op jit(solution)/shard_map/refine/pallas_call | solution.py:508
  90.8 1.9 %copy.17 = bf16[784,320]{0,1:T(8,128)(2,1)} copy(bf16[784,320]{0,1:T(8,128)(2,1)} %bitcast.9) | data formatting | bytes 1003520
  92.8 1.6 %copy.18 = f32[784,32]{0,1:T(8,128)} copy(f32[784,32]{0,1:T(8,128)} %bitcast.11) | data formatting | bytes 200704
